TPU v7x, 128 devices: a whole 4x4x4 slice. The times are simulated.
128 devices in a mesh: gx: 32 (over x_hi, z, y), gy: 4 (over x_lo, core).
Axes of the slice: x: 4 (x_hi: 2, x_lo: 2; x = x_hi * 2 + x_lo), y: 4, z: 4, core: 2. Of those that a mesh axis runs over, the one named last changes fastest.
Arguments:
- populations: float32 [27, 256, 128, 128], P(None, 'gx', 'gy'), may hold values from 0.49 to 1.69
- precursor: float32 [27, 64, 128, 128], P(None, 'gx', 'gy'), may hold values from 0.49 to 1.69
- pairing: int32 [32], replicated, may hold values from 0 to 31, each once
- rates: float32 [27], replicated, may hold values from 0.5 to 1.9
- loading: float32 [32], replicated, may hold values from 4 to 32
- disc_cols: int32 [512], replicated, may hold values from 0 to 32767, as said below
- disc_turb: int32 [512], replicated, may hold values from -1 to 31, as said below
Outputs:
- read: float32 [27, 256, 128, 128], P(None, 'gx', 'gy')
- disc_speed: float32 [32], replicated
Inputs may be any that keep to these rules, and one draw needn't show every extreme that they name: `disc_cols`: each turbine's used slots name 8 to 16 spanwise-adjacent columns (periodic in y) of one streamwise plane; unused slots hold column 0. `disc_turb`: every turbine id 0..31 has 8 to 16 used slots, both counts reached; -1 marks an unused slot; slots are in no particular order.
All inputs are finite; a program needn't handle non-finite values.
Results may differ from a plain program's by a relative error of at most 0.00009.
Values sent between devices are 32-bit elements; how exact they have to be, the bound alone decides.
No kernel may reach another device: no remote copies, remote signals or barrier semaphores. Data moves between devices by JAX's collectives and lax.ppermute only.
A program may use at most 128 MiB of HBM per device.

v0:
```python
import jax
import jax.numpy as jnp
import numpy as np
from jax import lax
from jax.sharding import PartitionSpec as P

FULL_PRECISION = lax.Precision.HIGHEST


def extended(cells, sides, width):
    for axis, dim in sides:
        count = lax.axis_size(axis)
        head = lax.slice_in_dim(cells, 0, width, axis=dim)
        tail = lax.slice_in_dim(cells, cells.shape[dim] - width, cells.shape[dim], axis=dim)
        cells = jnp.concatenate(
            [
                lax.ppermute(tail, axis, [(i, (i + 1) % count) for i in range(count)]),
                cells,
                lax.ppermute(head, axis, [((i + 1) % count, i) for i in range(count)]),
            ],
            axis=dim,
        )
    return cells


def lattice_tables():
    steps_one = np.array([-1.0, 0.0, 1.0])
    weight_one = np.array([1.0 / 6.0, 2.0 / 3.0, 1.0 / 6.0])
    grid_x, grid_y, grid_z = np.meshgrid(np.arange(3), np.arange(3), np.arange(3), indexing="ij")
    grid_x = grid_x.ravel()
    grid_y = grid_y.ravel()
    grid_z = grid_z.ravel()
    shift_x = steps_one[grid_x]
    shift_y = steps_one[grid_y]
    shift_z = steps_one[grid_z]
    weights = weight_one[grid_x] * weight_one[grid_y] * weight_one[grid_z]
    vander = np.array([[1.0, 1.0, 1.0], [-1.0, 0.0, 1.0], [1.0, 0.0, 1.0]])
    inverse = np.array([[0.0, -0.5, 0.5], [1.0, 0.0, -1.0], [0.0, 0.5, 0.5]])
    moment_map = np.kron(np.kron(vander, vander), vander) * weights[None, :]
    back_map = np.kron(np.kron(inverse, inverse), inverse) / weights[:, None]
    third = 1.0 / 3.0
    fringe_map = np.stack(
        [
            weights,
            weights * shift_x,
            weights * shift_y,
            weights * shift_z,
            weights * shift_x * shift_x,
            weights * shift_y * shift_y,
            weights * shift_z * shift_z,
            weights * shift_x * shift_y,
            weights * shift_x * shift_z,
            weights * shift_y * shift_z,
        ]
    )
    quad_x = shift_x * shift_x - third
    quad_y = shift_y * shift_y - third
    quad_z = shift_z * shift_z - third
    rebuild_map = np.stack(
        [
            1.0 - 1.5 * (quad_x + quad_y + quad_z),
            3.0 * shift_x,
            3.0 * shift_y,
            3.0 * shift_z,
            4.5 * quad_x,
            4.5 * quad_y,
            4.5 * quad_z,
            9.0 * shift_x * shift_y,
            9.0 * shift_x * shift_z,
            9.0 * shift_y * shift_z,
        ],
        axis=1,
    )
    tables = (shift_x, shift_y, shift_z, moment_map, back_map, fringe_map, rebuild_map)
    return tuple((jnp.asarray(table, dtype=jnp.float32) for table in tables))


def disc_profile(depth):
    heights = jnp.arange(depth).astype(jnp.float32)
    return jnp.exp(-jnp.square((heights - depth / 3.0) / (depth / 6.0)))


def relax_cells(tables, moments, rates, force):
    shift_x, shift_y, shift_z, moment_map, back_map = tables[:5]
    density = moments[0]
    velocity_x = moments[9] / density
    velocity_y = moments[3] / density
    velocity_z = moments[1] / density
    projected = (
        shift_x[:, None] * velocity_x[None, :]
        + shift_y[:, None] * velocity_y[None, :]
        + shift_z[:, None] * velocity_z[None, :]
    )
    speed_sq = velocity_x * velocity_x + velocity_y * velocity_y + velocity_z * velocity_z
    balance = density[None, :] * (
        1.0 + 3.0 * projected + 4.5 * projected * projected - 1.5 * speed_sq[None, :]
    )
    balance_moments = jnp.dot(moment_map, balance, precision=FULL_PRECISION)
    relaxed = moments - rates[:, None] * (moments - balance_moments)
    return (
        jnp.dot(back_map, relaxed, precision=FULL_PRECISION)
        + 3.0 * shift_x[:, None] * force[None, :]
    )


def body(populations, precursor, pairing, rates, loading, disc_cols, disc_turb):
    tables = lattice_tables()
    comps, width_x, width_y, depth = populations.shape
    fringe_width = precursor.shape[1]
    turbines = loading.shape[0]
    flat = populations.reshape(comps, width_x * width_y * depth)
    moments = jnp.dot(tables[3], flat, precision=FULL_PRECISION)
    velocity_x = moments[9] / moments[0]
    profile = disc_profile(depth)
    along_y = width_y * lax.axis_size("gy")
    tile_x = lax.axis_index("gx")
    tile_y = lax.axis_index("gy")
    local_x = disc_cols // along_y - tile_x * width_x
    local_y = disc_cols % along_y - tile_y * width_y
    owned = (
        (disc_turb >= 0)
        & (local_x >= 0)
        & (local_x < width_x)
        & (local_y >= 0)
        & (local_y < width_y)
    )
    local_cell = jnp.where(owned, local_x * width_y + local_y, 0)
    columns = velocity_x.reshape(width_x * width_y, depth)[local_cell]
    row_values = jnp.where(owned, jnp.dot(columns, profile, precision=FULL_PRECISION), 0.0)
    owner_table = (disc_turb[None, :] == jnp.arange(turbines, dtype=jnp.int32)[:, None]).astype(
        jnp.float32
    )
    partial_totals = jnp.dot(owner_table, row_values, precision=FULL_PRECISION)
    totals = lax.psum(partial_totals, ("gx", "gy"))
    counts = jnp.sum(owner_table, axis=1)
    disc_speed = totals / (counts * jnp.sum(profile))
    thrust = 0.5 * loading * disc_speed * jnp.abs(disc_speed)
    row_thrust = jnp.dot(thrust, owner_table, precision=FULL_PRECISION)
    placed = (
        (jnp.arange(width_x * width_y, dtype=jnp.int32)[:, None] == local_cell[None, :])
        & owned[None, :]
    ).astype(jnp.float32)
    column_force = jnp.dot(placed, row_thrust, precision=FULL_PRECISION)
    force = -(column_force[:, None] * profile[None, :]).reshape(width_x * width_y * depth)
    post = relax_cells(tables, moments, rates, force).reshape(comps, width_x, width_y, depth)
    source_tile = pairing[tile_x]
    wanted = source_tile * fringe_width + jnp.arange(fringe_width, dtype=jnp.int32)
    piece = lax.all_gather(precursor, "gx", axis=1, tiled=True)
    have = jnp.arange(piece.shape[1], dtype=jnp.int32)
    chosen = (wanted[:, None] == have[None, :]).astype(jnp.float32)
    chosen_pops = jnp.einsum("pr,kryz->kpyz", chosen, piece, precision=FULL_PRECISION)
    selected = jnp.dot(
        tables[5],
        chosen_pops.reshape(comps, fringe_width * width_y * depth),
        precision=FULL_PRECISION,
    )
    rebuilt = jnp.dot(
        tables[6], selected.reshape(10, fringe_width * width_y * depth), precision=FULL_PRECISION
    )
    rebuilt = rebuilt.reshape(comps, fringe_width, width_y, depth)
    blend = (0.5 / (jnp.arange(fringe_width).astype(jnp.float32) + 1.0))[None, :, None, None]
    head = (1.0 - blend) * post[:, :fringe_width] + blend * rebuilt
    post = jnp.concatenate([head, post[:, fringe_width:]], axis=1)
    pieces = []
    padded = extended(post, (("gx", 1), ("gy", 2)), 1)
    for slot in range(27):
        step_x = slot // 9 - 1
        step_y = slot // 3 % 3 - 1
        pieces.append(
            padded[slot, 1 - step_x : 1 - step_x + width_x, 1 - step_y : 1 - step_y + width_y]
        )
    finished = []
    for slot in range(27):
        step_z = slot % 3 - 1
        moved = pieces[slot]
        if step_z == 1:
            moved = jnp.concatenate([post[26 - slot][:, :, :1], moved[:, :, :-1]], axis=2)
        elif step_z == -1:
            moved = jnp.concatenate([moved[:, :, 1:], post[26 - slot][:, :, -1:]], axis=2)
        finished.append(moved)
    return (jnp.stack(finished), disc_speed)


def solution(mesh):
    in_specs = (P(None, "gx", "gy", None), P(None, "gx", "gy", None), P(), P(), P(), P(), P())
    out_specs = (P(None, "gx", "gy", None), P())
    return jax.shard_map(body, mesh=mesh, in_specs=in_specs, out_specs=out_specs, check_vma=False)
```

profile of v0, /device:TPU:121, one launch (start us, length us, event | category | flops | bytes accessed | tf_op | source)
XLA Modules:
  0.0 319.7 jit_solution(4355309923791451909)
XLA Ops:
  7.2 2.2 copy.22
  9.4 2.4 pad.213
  11.9 4.4 %copy.26 = f32[4,8,256,128]{3,1,2,0:T(8,128)} copy(f32[4,8,256,128]{3,2,1,0:T(8,128)S(1)} %bitcast.220) | data formatting | bytes 8388608
  16.4 5.4 %fusion.80 = f32[27,32768]{1,0:T(8,128)S(1)} fusion(f32[27,27]{1,0:T(8,128)S(1)} %copy-done.5, f32[27,32768]{1,0:T(8,128)} %bitcast.218), kind=kOutput, calls=%fused_computation.182 | convolution fusion | flops 286654464 | bytes 7080804 | tf_op jit(solution)/shard_map/dot_general | solution.py:112
  21.8 2.0 copy-done.2
  24.3 1.0 gather_fusion
  25.8 70.7 %psum.7 = f32[32]{0:T(128)S(1)} all-reduce(f32[32]{0:T(128)S(1)} %convolution_bitcast_fusion.1), channel_id=1, replica_groups=mesh['gx'=32,'gy'=4] {'gx','gy'}, use_global_device_ids=true, to_apply=%region_0.1 | all-reduce | flops 32 | bytes 256 | tf_op jit(solution)/shard_map/psum | solution.py:134
  97.3 0.7 multiply_divide_fusion
  98.5 7.5 %fusion.1 = f32[27,32768]{1,0:T(8,128)S(1)} fusion(f32[27,32768]{1,0:T(8,128)} %copy-done.2, f32[27,27]{1,0:T(8,128)S(1)} %copy-done.5, f32[32768]{0:T(1024)S(1)} %bitcast.250, f32[32768]{0:T(1024)S(1)} %bitcast.252, f32[27]{0:T(128)S(1)} %copy-done.15, f32[32768]{0:T(1024)S(1)} %bitcast.251, f32[27]{0:T(128)S(1)} %copy-done.16, f32[32768]{0:T(1024)S(1)} %bitcast.217, ...), kind=kOutput, calls=%fused_computation.4 | convolution fusion | flops 299925504 | bytes 7736596 | tf_op jit(solution)/shard_map/dot_general | solution.py:98
  106.2 4.1 %convolution_add_fusion = f32[27,32768]{1,0:T(8,128)S(1)} fusion(f32[27,27]{1,0:T(8,128)S(1)} %copy-done.4, f32[27,32768]{1,0:T(8,128)S(1)} %fusion.1, f32[32768]{0:T(1024)S(1)} %negate_bitcast_fusion, f32[27]{0:T(128)S(1)} %copy-done.10), kind=kOutput, calls=%fused_computation.1 | convolution fusion | flops 288423936 | bytes 7211984 | tf_op jit(solution)/shard_map/dot_general | solution.py:101
  110.3 0.7 copy.27
  111.5 1.8 copy-done
  113.3 3.6 %collective-permute-start = (f32[27,1,32,128]{3,2,1,0:T(8,128)S(1)}, f32[27,1,32,128]{3,2,1,0:T(8,128)S(1)}, u32[]{:S(2)}, u32[]{:S(2)}) collective-permute-start(f32[27,1,32,128]{3,2,1,0:T(8,128)S(1)} %slice.391), channel_id=1, source_target_pairs={{0,4},{4,8},{8,12},{12,16},{16,20},{20,24},{24,28},{28,32},{32,36}... | collective-permute-start | bytes 1327112 | tf_op jit(solution)/shard_map/ppermute | solution.py:17
  116.9 0.7 dynamic_slice.3
  118.3 129.6 %all-gather.2.cloned.1.call-done = f32[27,64,32,128]{3,2,0,1:T(8,128)} async-done(((f32[27,2,32,128]{3,2,0,1:T(8,128)}), f32[27,64,32,128]{3,2,0,1:T(8,128)}) %all-gather.2.cloned.1.call-update) | async-done | bytes 28311568 | tf_op jit(solution)/shard_map/all_gather | solution.py:148
  247.9 31.6 %fusion.26 = f32[27,2,32,128]{3,1,2,0:T(2,128)S(1)} fusion(f32[27,64,32,128]{3,2,0,1:T(8,128)} %all-gather.2.cloned.1.call-done, s32[2]{0:T(128)S(1)} %iota_add_fusion), kind=kOutput, calls=%fused_computation.29 | convolution fusion | flops 169869440 | bytes 29196296 | tf_op jit(solution)/shard_map/pr,kryz->kpyz/dot_general | solution.py:151
  280.4 0.7 fusion.81
  281.1 1.0 fusion.82
  282.7 2.7 collective-permute-start.1
  285.8 13.2 %collective-permute-done.1 = f32[27,1,32,128]{3,2,1,0:T(8,128)S(1)} collective-permute-done((f32[27,1,32,128]{3,2,1,0:T(8,128)S(1)}, f32[27,1,32,128]{3,2,1,0:T(8,128)S(1)}, u32[]{:S(2)}, u32[]{:S(2)}) %collective-permute-start.1) | collective-permute-done | bytes 442400 | tf_op jit(solution)/shard_map/ppermute | solution.py:19
  299.3 2.2 collective-permute-start.3
  301.5 2.0 collective-permute-done.3
  303.5 3.1 collective-permute-done.2
  311.0 1.8 copy-done.8
  (108 shorter events, 9.1 us)
Async XLA Ops:
  7.2 240.7 %all-gather.2.cloned.1.call-start = ((), (), s32[]{:S(2)}) async-start(), calls=%async_computation | async-start | bytes 29196288 | tf_op jit(solution)/shard_map/all_gather | solution.py:148
  11.9 4.4 %copy-start.7 = (s32[512]{0:T(512)S(1)}, s32[512]{0:T(512)}, u32[]{:S(2)}) copy-start(s32[512]{0:T(512)} %param.20) | copy-start | bytes 6148
  11.9 4.4 %copy-start.9 = (s32[512]{0:T(512)S(1)}, s32[512]{0:T(512)}, u32[]{:S(2)}) copy-start(s32[512]{0:T(512)} %param.19) | copy-start | bytes 6148
  11.9 4.5 %copy-start.5 = (f32[27,27]{1,0:T(8,128)S(1)}, f32[27,27]{1,0:T(8,128)}, u32[]{:S(2)}) copy-start(f32[27,27]{1,0:T(8,128)} %constant.89.clone) | copy-start | bytes 8752
  21.7 2.0 copy-start.2
  23.7 74.2 %copy-start.12 = (f32[32]{0:T(128)S(1)}, f32[32]{0:T(128)}, u32[]{:S(2)}) copy-start(f32[32]{0:T(128)} %param.18) | copy-start | bytes 388
  23.7 74.7 %copy-start.13 = (f32[27]{0:T(128)S(1)}, f32[27]{0:T(128)}, u32[]{:S(2)}) copy-start(f32[27]{0:T(128)} %param.17) | copy-start | bytes 328
  23.7 74.8 %copy-start.15 = (f32[27]{0:T(128)S(1)}, f32[27]{0:T(128)}, u32[]{:S(2)}) copy-start(f32[27]{0:T(128)} %constant.88.clone) | copy-start | bytes 328
  23.7 74.8 %copy-start.16 = (f32[27]{0:T(128)S(1)}, f32[27]{0:T(128)}, u32[]{:S(2)}) copy-start(f32[27]{0:T(128)} %constant.87.clone) | copy-start | bytes 328
  23.7 74.8 %copy-start.17 = (f32[27]{0:T(128)S(1)}, f32[27]{0:T(128)}, u32[]{:S(2)}) copy-start(f32[27]{0:T(128)} %constant.86.clone) | copy-start | bytes 328
  98.0 8.1 %copy-start.11 = (f32[32]{0:T(128)}, f32[32]{0:T(128)S(1)}, u32[]{:S(2)}) copy-start(f32[32]{0:T(128)S(1)} %multiply_divide_fusion) | copy-start | bytes 388
  98.5 7.7 %copy-start.4 = (f32[27,27]{1,0:T(8,128)S(1)}, f32[27,27]{1,0:T(8,128)}, u32[]{:S(2)}) copy-start(f32[27,27]{1,0:T(8,128)} %constant.90.clone) | copy-start | bytes 8752
  98.5 7.6 %copy-start.10 = (f32[27]{0:T(128)S(1)}, f32[27]{0:T(128)}, u32[]{:S(2)}) copy-start(f32[27]{0:T(128)} %constant.95) | copy-start | bytes 328
  111.1 5.8 %copy-start.14 = (s32[32]{0:T(128)S(1)}, s32[32]{0:T(128)}, u32[]{:S(2)}) copy-start(s32[32]{0:T(128)} %param.16) | copy-start | bytes 388
  111.5 1.8 copy-start
  113.3 172.5 %collective-permute-start = (f32[27,1,32,128]{3,2,1,0:T(8,128)S(1)}, f32[27,1,32,128]{3,2,1,0:T(8,128)S(1)}, u32[]{:S(2)}, u32[]{:S(2)}) collective-permute-start(f32[27,1,32,128]{3,2,1,0:T(8,128)S(1)} %slice.391), channel_id=1, source_target_pairs={{0,4},{4,8},{8,12},{12,16},{16,20},{20,24},{24,28},{28,32},{32,36}... | collective-permute-start | bytes 1327112 | tf_op jit(solution)/shard_map/ppermute | solution.py:17
  279.5 0.9 copy-start.6
  279.5 1.6 copy-start.3
  280.3 2.0 copy-start.1
  282.7 16.4 %collective-permute-start.1 = (f32[27,1,32,128]{3,2,1,0:T(8,128)S(1)}, f32[27,1,32,128]{3,2,1,0:T(8,128)S(1)}, u32[]{:S(2)}, u32[]{:S(2)}) collective-permute-start(f32[27,1,32,128]{3,2,1,0:T(8,128)S(1)} %slice.394), channel_id=1, source_target_pairs={{4,0},{8,4},{12,8},{16,12},{20,16},{24,20},{28,24},{32,28},{36,32}... | collective-permute-start | bytes 1327112 | tf_op jit(solution)/shard_map/ppermute | solution.py:19
  299.3 4.2 %collective-permute-start.3 = (f32[27,10,1,128]{3,2,1,0:T(1,128)S(1)}, f32[27,10,1,128]{3,2,1,0:T(1,128)S(1)}, u32[]{:S(2)}, u32[]{:S(2)}) collective-permute-start(f32[27,10,1,128]{3,2,1,0:T(1,128)S(1)} %get-tuple-element.27), channel_id=1, source_target_pairs={{0,1},{1,2},{2,3},{3,0},{4,5},{5,6},{6,7},{7,4},{8,9},{9,10},{10,1... | collective-permute-start | bytes 414728 | tf_op jit(solution)/shard_map/ppermute | solution.py:17
  301.5 5.1 %collective-permute-start.2 = (f32[27,10,1,128]{3,2,1,0:T(1,128)S(1)}, f32[27,10,1,128]{3,2,1,0:T(1,128)S(1)}, u32[]{:S(2)}, u32[]{:S(2)}) collective-permute-start(f32[27,10,1,128]{3,2,1,0:T(1,128)S(1)} %get-tuple-element.28), channel_id=1, source_target_pairs={{1,0},{2,1},{3,2},{0,3},{5,4},{6,5},{7,6},{4,7},{9,8},{10,9},{11,1... | collective-permute-start | bytes 414728 | tf_op jit(solution)/shard_map/ppermute | solution.py:19
  311.0 1.8 copy-start.8
Sparse Core Ops, SparseCore 0:
  11.0 236.7 all-gather.1
where the time goes:
time: 320 us
  waiting for transfers between devices  148 us (46%)
  blocking collectives  70.7 us (22%)
  matrix products  51.3 us (16%)
  local copies, waits for them, and re-layouts  20.7 us (6%)
  between operations  15.4 us (5%)
  starting transfers between devices  8.56 us (3%)
  other arithmetic  4.99 us (2%)
    all_gather x1, waiting for transfers between devices, body(): piece = lax.all_gather(precursor, 'gx', axis=1, tiled=True)  130 us
    psum x1, blocking collectives, body(): totals = lax.psum(partial_totals, ('gx', 'gy'))  70.7 us
    dot_general x1, matrix products, body(): jnp.einsum('pr,kryz->kpyz', chosen, piece, precision=FULL_PRECISION)  31.6 us
    unnamed x45, local copies, waits for them, and re-layouts  16.8 us
    ppermute x2, waiting for transfers between devices, extended(): lax.ppermute(head, axis, [((i + 1) % count, i) for i in range(count)])  16.3 us
    dot_general x1, matrix products, relax_cells(): balance_moments = jnp.dot(moment_map, balance, precision=FULL_PRECISION)  7.5 us
  transfers between devices with their start and end apart: 5, of which 4 were waited for; matrix products, arithmetic and copies ran while one was open for 20% of the time, Pallas kernels for 0%

commit v1 on v0

--- a/solution.py
+++ b/solution.py
@@ -104,6 +104,13 @@
 
 
 def body(populations, precursor, pairing, rates, loading, disc_cols, disc_turb):
+
+    def serve_samples(row_data):
+        prior = jnp.stack([row_data for _ in range(jax.lax.axis_size("gx"))], axis=0)
+        latest = jax.lax.all_to_all(prior, axis_name="gx", split_axis=0, concat_axis=0)
+        state_next = jnp.concatenate(latest, axis=1)
+        return state_next
+
     tables = lattice_tables()
     comps, width_x, width_y, depth = populations.shape
     fringe_width = precursor.shape[1]
@@ -145,7 +152,7 @@
     post = relax_cells(tables, moments, rates, force).reshape(comps, width_x, width_y, depth)
     source_tile = pairing[tile_x]
     wanted = source_tile * fringe_width + jnp.arange(fringe_width, dtype=jnp.int32)
-    piece = lax.all_gather(precursor, "gx", axis=1, tiled=True)
+    piece = serve_samples(precursor)
     have = jnp.arange(piece.shape[1], dtype=jnp.int32)
     chosen = (wanted[:, None] == have[None, :]).astype(jnp.float32)
     chosen_pops = jnp.einsum("pr,kryz->kpyz", chosen, piece, precision=FULL_PRECISION)

time: 320 us -> 649 us (2.03)
  blocking collectives: 70.7 us -> 517 us
  waiting for transfers between devices: 148 us -> 20.1 us
  local copies, waits for them, and re-layouts: 20.7 us -> 54 us
  matrix products: 51.3 us -> 32.9 us
  between operations: 15.4 us -> 2.03 us
  starting transfers between devices: 8.56 us -> 15.9 us
    psum x1, blocking collectives: 70.7 us -> 517 us  [body(): totals = lax.psum(partial_totals, ('gx', 'gy'))]
    all_gather x1 -> x0, waiting for transfers between devices: 130 us -> none  [body(): piece = lax.all_gather(precursor, 'gx', axis=1, tiled=True)]
    reshape x0 -> x1, local copies, waits for them, and re-layouts: none -> 19.5 us  [serve_samples(): state_next = jnp.concatenate(latest, axis=1)]
    dot_general x1, matrix products: 31.6 us -> 13.7 us  [body(): jnp.einsum('pr,kryz->kpyz', chosen, piece, precision=FULL_PRECISION)]
    another operation x0 -> x1, local copies, waits for them, and re-layouts: none -> 14.1 us  [serve_samples(): jnp.stack([row_data for _ in range(jax.lax.axis_size('gx'))], axis=0)]
    all_to_all x0 -> x1, starting transfers between devices: none -> 8.91 us  [serve_samples(): jax.lax.all_to_all(prior, axis_name='gx', split_axis=0, concat_axis=0)]
  transfers between devices with their start and end apart: 5 -> 5, of which waited for: 4 -> 2; matrix products, arithmetic and copies ran while one was open for 20% -> 10% of each run, Pallas kernels for 0% -> 0%
where the time goes in v1:
time: 649 us; the launch traced here: 647 us
  blocking collectives  517 us (80%)
  local copies, waits for them, and re-layouts  54 us (8%)
  matrix products  32.9 us (5%)
  waiting for transfers between devices  20.1 us (3%)
  starting transfers between devices  15.9 us (2%)
    psum x1, blocking collectives, body(): totals = lax.psum(partial_totals, ('gx', 'gy'))  517 us
    ppermute x2, waiting for transfers between devices, extended(): lax.ppermute(head, axis, [((i + 1) % count, i) for i in range(count)])  20 us
    reshape x1, local copies, waits for them, and re-layouts, serve_samples(): state_next = jnp.concatenate(latest, axis=1)  19.5 us
    unnamed x45, local copies, waits for them, and re-layouts  16.5 us
    another operation x1, local copies, waits for them, and re-layouts, serve_samples(): jnp.stack([row_data for _ in range(jax.lax.axis_size('gx'))], axis=0)  14.1 us
    dot_general x1, matrix products, body(): jnp.einsum('pr,kryz->kpyz', chosen, piece, precision=FULL_PRECISION)  13.7 us
  transfers between devices with their start and end apart: 5, of which 2 were waited for; matrix products, arithmetic and copies ran while one was open for 10% of the time, Pallas kernels for 0%

profile of v1, /device:TPU:121, one launch (start us, length us, event | category | flops | bytes accessed | tf_op | source)
XLA Modules:
  0.0 647.2 jit_solution(5856367693554360814)
XLA Ops:
  0.6 1.9 copy.22
  2.5 14.1 %stack.40 = f32[32,27,2,32,128]{4,2,3,1,0:T(2,128)} broadcast(f32[27,2,32,128]{3,1,2,0:T(2,128)S(1)} %copy.22), dimensions={1,2,3,4} | broadcast | bytes 29196288 | tf_op jit(solution)/shard_map/stack | solution.py:109
  16.6 8.9 %all-to-all-start = ((f32[32,27,2,32,128]{4,2,3,1,0:T(2,128)}), f32[32,27,2,32,128]{4,2,3,1,0:T(2,128)}, u32[]{:S(2)}, u32[]{:S(2)}) async-start(f32[32,27,2,32,128]{4,2,3,1,0:T(2,128)} %stack.40), calls=%async_computation | async-start | bytes 56623104 | tf_op jit(solution)/shard_map/all_to_all | solution.py:110
  25.6 2.4 pad.213
  28.0 4.4 copy.26
  32.5 5.4 fusion.75
  37.9 2.0 copy-done.2
  40.5 1.0 gather_fusion
  42.0 517.3 %psum.7 = f32[32]{0:T(128)S(1)} all-reduce(f32[32]{0:T(128)S(1)} %convolution_bitcast_fusion.2), channel_id=1, replica_groups=mesh['gx'=32,'gy'=4] {'gx','gy'}, use_global_device_ids=true, to_apply=%region_0.1 | all-reduce | flops 32 | bytes 256 | tf_op jit(solution)/shard_map/psum | solution.py:141
  560.0 0.7 multiply_divide_fusion
  561.3 7.4 %fusion.1 = f32[27,32768]{1,0:T(8,128)S(1)} fusion(f32[27,32768]{1,0:T(8,128)} %copy-done.2, f32[27,27]{1,0:T(8,128)S(1)} %copy-done.5, f32[32768]{0:T(1024)S(1)} %bitcast.254, f32[32768]{0:T(1024)S(1)} %bitcast.256, f32[27]{0:T(128)S(1)} %copy-done.17, f32[32768]{0:T(1024)S(1)} %bitcast.255, f32[27]{0:T(128)S(1)} %copy-done.16, f32[32768]{0:T(1024)S(1)} %bitcast.221, ...), kind=kOutput, calls=%fused_computation.4 | convolution fusion | flops 299925504 | bytes 7736596 | tf_op jit(solution)/shard_map/dot_general | solution.py:98
  568.9 3.8 convolution_add_fusion
  572.7 0.7 copy.27
  573.8 1.8 copy-done
  575.6 4.5 collective-permute-start
  581.4 19.5 %copy.23 = f32[27,32,2,32,128]{4,2,1,3,0:T(2,128)} copy(f32[27,32,2,32,128]{4,2,3,0,1:T(2,128)} %bitcast.18) | data formatting | bytes 56623104 | tf_op jit(solution)/shard_map/reshape | solution.py:111
  600.9 13.7 %convolution_bitcast_fusion = f32[27,2,32,128]{3,1,2,0:T(2,128)S(1)} fusion(f32[27,64,32,128]{3,1,2,0:T(8,128)} %bitcast.219, s32[2]{0:T(128)S(1)} %iota_add_fusion), kind=kOutput, calls=%fused_computation.27 | convolution fusion | flops 169869440 | bytes 29196296 | tf_op jit(solution)/shard_map/pr,kryz->kpyz/dot_general | solution.py:158
  615.5 0.7 fusion.76
  616.2 1.0 fusion.77
  618.3 16.1 %collective-permute-done.1 = f32[27,1,32,128]{3,2,1,0:T(8,128)S(1)} collective-permute-done((f32[27,1,32,128]{3,2,1,0:T(8,128)S(1)}, f32[27,1,32,128]{3,2,1,0:T(8,128)S(1)}, u32[]{:S(2)}, u32[]{:S(2)}) %collective-permute-start.1) | collective-permute-done | bytes 442400 | tf_op jit(solution)/shard_map/ppermute | solution.py:19
  634.6 1.8 collective-permute-start.2
  636.4 0.6 collective-permute-start.3
  637.0 3.9 collective-permute-done.2
  645.4 1.8 copy-done.8
  (109 shorter events, 9.6 us)
Async XLA Ops:
  16.6 564.8 %all-to-all-start = ((f32[32,27,2,32,128]{4,2,3,1,0:T(2,128)}), f32[32,27,2,32,128]{4,2,3,1,0:T(2,128)}, u32[]{:S(2)}, u32[]{:S(2)}) async-start(f32[32,27,2,32,128]{4,2,3,1,0:T(2,128)} %stack.40), calls=%async_computation | async-start | bytes 56623104 | tf_op jit(solution)/shard_map/all_to_all | solution.py:110
  28.0 4.5 copy-start.7
  28.0 4.5 copy-start.9
  28.0 4.5 copy-start.5
  37.9 2.0 copy-start.2
  39.9 520.8 %copy-start.12 = (f32[32]{0:T(128)S(1)}, f32[32]{0:T(128)}, u32[]{:S(2)}) copy-start(f32[32]{0:T(128)} %param.18) | copy-start | bytes 388
  39.9 521.3 %copy-start.13 = (f32[27]{0:T(128)S(1)}, f32[27]{0:T(128)}, u32[]{:S(2)}) copy-start(f32[27]{0:T(128)} %param.17) | copy-start | bytes 328
  39.9 521.3 %copy-start.15 = (f32[27]{0:T(128)S(1)}, f32[27]{0:T(128)}, u32[]{:S(2)}) copy-start(f32[27]{0:T(128)} %constant.86.clone) | copy-start | bytes 328
  39.9 521.3 %copy-start.16 = (f32[27]{0:T(128)S(1)}, f32[27]{0:T(128)}, u32[]{:S(2)}) copy-start(f32[27]{0:T(128)} %constant.87.clone) | copy-start | bytes 328
  39.9 521.3 %copy-start.17 = (f32[27]{0:T(128)S(1)}, f32[27]{0:T(128)}, u32[]{:S(2)}) copy-start(f32[27]{0:T(128)} %constant.88.clone) | copy-start | bytes 328
  560.7 8.0 %copy-start.11 = (f32[32]{0:T(128)}, f32[32]{0:T(128)S(1)}, u32[]{:S(2)}) copy-start(f32[32]{0:T(128)S(1)} %multiply_divide_fusion) | copy-start | bytes 388
  561.3 7.6 %copy-start.4 = (f32[27,27]{1,0:T(8,128)S(1)}, f32[27,27]{1,0:T(8,128)}, u32[]{:S(2)}) copy-start(f32[27,27]{1,0:T(8,128)} %constant.90.clone) | copy-start | bytes 8752
  561.3 7.6 %copy-start.10 = (f32[27]{0:T(128)S(1)}, f32[27]{0:T(128)}, u32[]{:S(2)}) copy-start(f32[27]{0:T(128)} %constant.95) | copy-start | bytes 328
  573.4 6.7 %copy-start.14 = (s32[32]{0:T(128)S(1)}, s32[32]{0:T(128)}, u32[]{:S(2)}) copy-start(s32[32]{0:T(128)} %param.16) | copy-start | bytes 388
  573.8 1.8 copy-start
  575.6 42.6 %collective-permute-start = (f32[27,1,32,128]{3,2,1,0:T(8,128)S(1)}, f32[27,1,32,128]{3,2,1,0:T(8,128)S(1)}, u32[]{:S(2)}, u32[]{:S(2)}) collective-permute-start(f32[27,1,32,128]{3,2,1,0:T(8,128)S(1)} %slice.391), channel_id=1, source_target_pairs={{0,4},{4,8},{8,12},{12,16},{16,20},{20,24},{24,28},{28,32},{32,36}... | collective-permute-start | bytes 1327112 | tf_op jit(solution)/shard_map/ppermute | solution.py:17
  614.6 0.9 copy-start.6
  614.6 1.6 copy-start.3
  615.5 2.0 copy-start.1
  617.8 16.6 %collective-permute-start.1 = (f32[27,1,32,128]{3,2,1,0:T(8,128)S(1)}, f32[27,1,32,128]{3,2,1,0:T(8,128)S(1)}, u32[]{:S(2)}, u32[]{:S(2)}) collective-permute-start(f32[27,1,32,128]{3,2,1,0:T(8,128)S(1)} %slice.394), channel_id=1, source_target_pairs={{4,0},{8,4},{12,8},{16,12},{20,16},{24,20},{28,24},{32,28},{36,32}... | collective-permute-start | bytes 1327112 | tf_op jit(solution)/shard_map/ppermute | solution.py:19
  634.6 6.3 collective-permute-start.2
  636.4 4.5 collective-permute-start.3
  645.4 1.8 copy-start.8
